TPU v7x, 512 devices: a whole 4x4x16 slice. The times are simulated.
512 devices in a mesh: blk: 64 (over x_hi, z, core), tgt: 8 (over y, x_lo).
Axes of the slice: x: 4 (x_hi: 2, x_lo: 2; x = x_hi * 2 + x_lo), y: 4, z: 16, core: 2. Of those that a mesh axis runs over, the one named last changes fastest.
Arguments:
- queries: bfloat16 [65536, 1024], P(('blk', 'tgt')), may hold values from -6 to 6
- keys: bfloat16 [4096, 1024], P('blk'), may hold values from -6 to 6
- values: bfloat16 [4096, 1024], P('blk'), may hold values from -6 to 6
- out_weight: bfloat16 [1024, 1024], P('tgt'), may hold values from -0.1875 to 0.1875
- out_grad: bfloat16 [65536, 1024], P(('blk', 'tgt')), may hold values from -24 to 24
Outputs:
- outputs: bfloat16 [65536, 1024], P(('blk', 'tgt'))
- query_grad: bfloat16 [65536, 1024], P(('blk', 'tgt'))
- key_grad: bfloat16 [4096, 1024], P('blk', 'tgt')
- value_grad: bfloat16 [4096, 1024], P('blk', 'tgt')
- weight_grad: bfloat16 [1024, 1024], P('tgt', 'blk')
All inputs are finite; a program needn't handle non-finite values.
Results may differ from a plain program's by a relative error of at most 0.017.
Values may be sent and summed in bfloat16 or wider, within the bound.
No kernel may reach another device: no remote copies, remote signals or barrier semaphores. Data moves between devices by JAX's collectives and lax.ppermute only.
A program may use at most 64 MiB of HBM per device.

v0:
```python
import jax
import jax.numpy as jnp
from jax import lax
from jax.sharding import PartitionSpec as P

D = 1024
HEADS = 16
HD = 64
WIN = 5
SRC_DEV = 64


def shifted(value, axis, steps):
    count = lax.axis_size(axis)
    pairs = [(source, (source + steps) % count) for source in range(count)]
    return lax.ppermute(value, axis, pairs)


def for_sending(value):
    return jax.tree.map(lambda a: a.astype(jnp.bfloat16) if a.dtype == jnp.float32 else a, value)


def head_block(query_cols, key_cols, value_cols, grad_cols, group_heads):
    scale = HD ** (-0.5)
    count = query_cols.shape[0]
    width = key_cols.shape[0]
    query_heads = query_cols.reshape(count, group_heads, HD)
    key_heads = key_cols.reshape(width, group_heads, HD)
    value_heads = value_cols.reshape(width, group_heads, HD)
    grad_heads = grad_cols.reshape(count, group_heads, HD)
    scores = (
        jnp.einsum("rhd,jhd->hrj", query_heads, key_heads, preferred_element_type=jnp.float32)
        * scale
    )
    top = jnp.max(scores, axis=-1, keepdims=True)
    expo = jnp.exp(scores - top)
    probs = expo / jnp.sum(expo, axis=-1, keepdims=True)
    probs_low = probs.astype(jnp.bfloat16)
    attended = jnp.einsum(
        "hrj,jhd->rhd", probs_low, value_heads, preferred_element_type=jnp.float32
    )
    attended = attended.reshape(count, group_heads * HD).astype(jnp.bfloat16)
    prob_grad = jnp.einsum(
        "rhd,jhd->hrj", grad_heads, value_heads, preferred_element_type=jnp.float32
    )
    center = jnp.sum(probs * prob_grad, axis=-1, keepdims=True)
    score_grad = (scale * probs * (prob_grad - center)).astype(jnp.bfloat16)
    query_grad = jnp.einsum(
        "hrj,jhd->rhd", score_grad, key_heads, preferred_element_type=jnp.float32
    )
    query_grad = query_grad.reshape(count, group_heads * HD).astype(jnp.bfloat16)
    key_part = jnp.einsum(
        "hrj,rhd->jhd", score_grad, query_heads, preferred_element_type=jnp.float32
    )
    value_part = jnp.einsum(
        "hrj,rhd->jhd", probs_low, grad_heads, preferred_element_type=jnp.float32
    )
    return (
        attended,
        query_grad,
        key_part.reshape(width, group_heads * HD),
        value_part.reshape(width, group_heads * HD),
    )


def local(queries, keys, values, out_weight, out_grad):
    full_weight = lax.all_gather(out_weight, "tgt", axis=0, tiled=True)
    current = (keys, values)
    key_list = [keys]
    value_list = [values]
    for step in range(1, WIN):
        current = shifted((current[0], current[1]), "blk", 1)
        key_list.append(current[0])
        value_list.append(current[1])
    seen_keys = jnp.concatenate(key_list, axis=0)
    seen_values = jnp.concatenate(value_list, axis=0)
    attended_grad = jnp.dot(out_grad, full_weight.T, preferred_element_type=jnp.float32).astype(
        jnp.bfloat16
    )
    group_heads = min(4, HEADS)
    span = group_heads * HD
    pieces = []
    for first in range(0, D, span):
        pieces.append(
            head_block(
                queries[:, first : first + span],
                seen_keys[:, first : first + span],
                seen_values[:, first : first + span],
                attended_grad[:, first : first + span],
                group_heads,
            )
        )
    attended = jnp.concatenate([p[0] for p in pieces], axis=1)
    query_grad = jnp.concatenate([p[1] for p in pieces], axis=1)
    key_part = jnp.concatenate([p[2] for p in pieces], axis=1)
    value_part = jnp.concatenate([p[3] for p in pieces], axis=1)
    outputs = jnp.dot(attended, full_weight, preferred_element_type=jnp.float32).astype(
        jnp.bfloat16
    )
    rows = SRC_DEV
    carried = (key_part[(WIN - 1) * rows : WIN * rows], value_part[(WIN - 1) * rows : WIN * rows])
    for step in range(WIN - 2, -1, -1):
        moved = shifted((for_sending(carried[0]), for_sending(carried[1])), "blk", -1)
        carried = (
            moved[0] + key_part[step * rows : (step + 1) * rows],
            moved[1] + value_part[step * rows : (step + 1) * rows],
        )
    key_total, value_total = carried
    key_grad, value_grad = (
        lax.psum_scatter(
            key_total.astype(jnp.bfloat16), "tgt", scatter_dimension=1, tiled=True
        ).astype(jnp.float32),
        lax.psum_scatter(
            value_total.astype(jnp.bfloat16), "tgt", scatter_dimension=1, tiled=True
        ).astype(jnp.float32),
    )
    tile_sum = lax.psum_scatter(
        jnp.einsum("rc,re->ce", attended, out_grad, preferred_element_type=jnp.float32).astype(
            jnp.bfloat16
        ),
        "tgt",
        scatter_dimension=0,
        tiled=True,
    ).astype(jnp.float32)
    weight_grad = lax.psum_scatter(tile_sum, "blk", scatter_dimension=1, tiled=True)
    return (
        outputs,
        query_grad,
        key_grad.astype(jnp.bfloat16),
        value_grad.astype(jnp.bfloat16),
        weight_grad.astype(jnp.bfloat16),
    )


def solution(mesh):
    return jax.shard_map(
        local,
        mesh=mesh,
        in_specs=(
            P(("blk", "tgt"), None),
            P("blk", None),
            P("blk", None),
            P("tgt", None),
            P(("blk", "tgt"), None),
        ),
        out_specs=(
            P(("blk", "tgt"), None),
            P(("blk", "tgt"), None),
            P("blk", "tgt"),
            P("blk", "tgt"),
            P("tgt", "blk"),
        ),
        check_vma=False,
    )
```

profile of v0, /device:TPU:8, one launch (start us, length us, event | category | flops | bytes accessed | tf_op | source)
XLA Modules:
  0.0 457.7 jit_solution(14117293037007560445)
XLA Ops:
  8.0 1.9 collective-permute-start.4
  9.9 3.9 collective-permute-start
  17.1 7.0 %collective-permute-done.4 = bf16[64,1024]{1,0:T(8,128)(2,1)S(1)} collective-permute-done((bf16[64,1024]{1,0:T(8,128)(2,1)}, bf16[64,1024]{1,0:T(8,128)(2,1)S(1)}, u32[]{:S(2)}, u32[]{:S(2)}) %collective-permute-start.4) | collective-permute-done | bytes 131104 | tf_op jit(solution)/shard_map/ppermute | solution.py:16
  24.1 1.9 collective-permute-start.5
  26.1 1.9 collective-permute-start.1
  28.0 6.0 %collective-permute-done.5 = bf16[64,1024]{1,0:T(8,128)(2,1)S(1)} collective-permute-done((bf16[64,1024]{1,0:T(8,128)(2,1)S(1)}, bf16[64,1024]{1,0:T(8,128)(2,1)S(1)}, u32[]{:S(2)}, u32[]{:S(2)}) %collective-permute-start.5) | collective-permute-done | bytes 131104 | tf_op jit(solution)/shard_map/ppermute | solution.py:16
  34.0 1.9 collective-permute-start.6
  36.1 1.9 collective-permute-start.2
  38.0 6.0 %collective-permute-done.6 = bf16[64,1024]{1,0:T(8,128)(2,1)S(1)} collective-permute-done((bf16[64,1024]{1,0:T(8,128)(2,1)S(1)}, bf16[64,1024]{1,0:T(8,128)(2,1)S(1)}, u32[]{:S(2)}, u32[]{:S(2)}) %collective-permute-start.6) | collective-permute-done | bytes 131104 | tf_op jit(solution)/shard_map/ppermute | solution.py:16
  44.0 1.9 collective-permute-start.7
  46.0 1.9 collective-permute-start.3
  48.0 6.0 %collective-permute-done.7 = bf16[64,1024]{1,0:T(8,128)(2,1)S(1)} collective-permute-done((bf16[64,1024]{1,0:T(8,128)(2,1)S(1)}, bf16[64,1024]{1,0:T(8,128)(2,1)S(1)}, u32[]{:S(2)}, u32[]{:S(2)}) %collective-permute-start.7) | collective-permute-done | bytes 131104 | tf_op jit(solution)/shard_map/ppermute | solution.py:16
  63.3 2.0 convolution_convert_fusion
  65.4 14.1 %all-gather.2.cloned.1.call-done = bf16[1024,1024]{1,0:T(8,128)(2,1)} async-done(((bf16[128,1024]{1,0:T(8,128)(2,1)}), bf16[1024,1024]{1,0:T(8,128)(2,1)}) %all-gather.2.cloned.1.call-update) | async-done | bytes 2097168 | tf_op jit(solution)/shard_map/all_gather | solution.py:67
  79.5 2.4 convolution_convert_fusion.1
  88.9 1.5 multiply_reduce_fusion.1
  97.9 2.1 collective-permute-start.12
  104.3 1.9 collective-permute-start.8
  107.2 3.9 collective-permute-start.13
  111.2 5.1 %collective-permute-start.9 = (bf16[64,1024]{1,0:T(8,128)(2,1)S(1)}, bf16[64,1024]{1,0:T(8,128)(2,1)S(1)}, u32[]{:S(2)}, u32[]{:S(2)}) collective-permute-start(bf16[64,1024]{1,0:T(8,128)(2,1)S(1)} %fusion.23), channel_id=1, source_target_pairs={{0,504},{8,0},{16,8},{24,16},{32,24},{40,32},{48,40},{56,48},{64,5... | collective-permute-start | bytes 393224 | tf_op jit(solution)/shard_map/ppermute | solution.py:16
  116.3 4.8 %collective-permute-start.14 = (bf16[64,1024]{1,0:T(8,128)(2,1)S(1)}, bf16[64,1024]{1,0:T(8,128)(2,1)S(1)}, u32[]{:S(2)}, u32[]{:S(2)}) collective-permute-start(bf16[64,1024]{1,0:T(8,128)(2,1)S(1)} %fusion.18), channel_id=1, source_target_pairs={{0,504},{8,0},{16,8},{24,16},{32,24},{40,32},{48,40},{56,48},{64,5... | collective-permute-start | bytes 393224 | tf_op jit(solution)/shard_map/ppermute | solution.py:16
  121.2 5.1 %collective-permute-start.10 = (bf16[64,1024]{1,0:T(8,128)(2,1)S(1)}, bf16[64,1024]{1,0:T(8,128)(2,1)S(1)}, u32[]{:S(2)}, u32[]{:S(2)}) collective-permute-start(bf16[64,1024]{1,0:T(8,128)(2,1)S(1)} %fusion.22), channel_id=1, source_target_pairs={{0,504},{8,0},{16,8},{24,16},{32,24},{40,32},{48,40},{56,48},{64,5... | collective-permute-start | bytes 393224 | tf_op jit(solution)/shard_map/ppermute | solution.py:16
  126.3 4.8 %collective-permute-start.15 = (bf16[64,1024]{1,0:T(8,128)(2,1)S(1)}, bf16[64,1024]{1,0:T(8,128)(2,1)S(1)}, u32[]{:S(2)}, u32[]{:S(2)}) collective-permute-start(bf16[64,1024]{1,0:T(8,128)(2,1)S(1)} %fusion.17), channel_id=1, source_target_pairs={{0,504},{8,0},{16,8},{24,16},{32,24},{40,32},{48,40},{56,48},{64,5... | collective-permute-start | bytes 393224 | tf_op jit(solution)/shard_map/ppermute | solution.py:16
  131.9 5.1 %collective-permute-start.11 = (bf16[64,1024]{1,0:T(8,128)(2,1)}, bf16[64,1024]{1,0:T(8,128)(2,1)}, u32[]{:S(2)}, u32[]{:S(2)}) collective-permute-start(bf16[64,1024]{1,0:T(8,128)(2,1)} %fusion.21), channel_id=1, source_target_pairs={{0,504},{8,0},{16,8},{24,16},{32,24},{40,32},{48,40},{56,48},{64,5... | collective-permute-start | bytes 393224 | tf_op jit(solution)/shard_map/ppermute | solution.py:16
  137.7 1.8 copy.103
  144.6 1.9 copy.105
  148.2 1.6 pad_maximum_fusion.3
  151.1 35.5 %reduce-scatter.15.cloned.1.call-done = bf16[128,64]{1,0:T(8,128)(2,1)} async-done(((bf16[1024,64]{1,0:T(8,128)(2,1)}), bf16[128,64]{1,0:T(8,128)(2,1)}) %reduce-scatter.15.cloned.1.call-update) | async-done | bytes 16400
  186.5 1.4 copy.104
  188.0 45.3 %reduce-scatter.13.cloned.1.call-done = bf16[128,64]{1,0:T(8,128)(2,1)} async-done(((bf16[1024,64]{1,0:T(8,128)(2,1)}), bf16[128,64]{1,0:T(8,128)(2,1)}) %reduce-scatter.13.cloned.1.call-update) | async-done | bytes 16400
  233.3 1.4 copy.102
  234.8 214.9 %reduce-scatter.17.cloned.1.call-done = f32[16,128]{1,0:T(8,128)} async-done(((f32[1024,128]{1,0:T(8,128)}), f32[16,128]{1,0:T(8,128)}) %reduce-scatter.17.cloned.1.call-update) | async-done | bytes 8208
  (190 shorter events, 43.9 us)
Async XLA Ops:
  7.2 56.1 %copy-start = (bf16[128,1024]{1,0:T(8,128)(2,1)S(1)}, bf16[128,1024]{1,0:T(8,128)(2,1)}, u32[]{:S(2)}) copy-start(bf16[128,1024]{1,0:T(8,128)(2,1)} %param.9) | copy-start | bytes 786436
  7.2 72.3 %all-gather.2.cloned.1.call-start = ((), (), s32[]{:S(2)}) async-start(), calls=%async_computation.4 | async-start | bytes 2359296 | tf_op jit(solution)/shard_map/all_gather | solution.py:67
  7.9 136.6 %reduce-scatter.11.cloned.1.call-start = ((), (), s32[]{:S(2)}) async-start(), calls=%async_computation.5 | async-start | bytes 2359296 | tf_op jit(solution)/shard_map/reduce_scatter | solution.py:117
  8.0 16.2 %collective-permute-start.4 = (bf16[64,1024]{1,0:T(8,128)(2,1)}, bf16[64,1024]{1,0:T(8,128)(2,1)S(1)}, u32[]{:S(2)}, u32[]{:S(2)}) collective-permute-start(bf16[64,1024]{1,0:T(8,128)(2,1)} %param.6), channel_id=1, source_target_pairs={{0,8},{8,16},{16,24},{24,32},{32,40},{40,48},{48,56},{56,64},{64,7... | collective-permute-start | bytes 393224 | tf_op jit(solution)/shard_map/ppermute | solution.py:16
  9.9 16.2 %collective-permute-start = (bf16[64,1024]{1,0:T(8,128)(2,1)}, bf16[64,1024]{1,0:T(8,128)(2,1)S(1)}, u32[]{:S(2)}, u32[]{:S(2)}) collective-permute-start(bf16[64,1024]{1,0:T(8,128)(2,1)} %param.7), channel_id=1, source_target_pairs={{0,8},{8,16},{16,24},{24,32},{32,40},{40,48},{48,56},{56,64},{64,7... | collective-permute-start | bytes 393224 | tf_op jit(solution)/shard_map/ppermute | solution.py:16
  16.7 79.4 %copy-start.24 = (bf16[128,256]{0,1:T(8,128)(2,1)}, bf16[128,256]{0,1:T(8,128)(2,1)S(1)}, u32[]{:S(2)}) copy-start(bf16[128,256]{0,1:T(8,128)(2,1)S(1)} %copy.74) | copy-start | bytes 196612
  17.1 42.6 %copy-start.26 = (bf16[128,256]{0,1:T(8,128)(2,1)}, bf16[128,256]{0,1:T(8,128)(2,1)S(1)}, u32[]{:S(2)}) copy-start(bf16[128,256]{0,1:T(8,128)(2,1)S(1)} %copy.80) | copy-start | bytes 196612
  24.1 9.9 %collective-permute-start.5 = (bf16[64,1024]{1,0:T(8,128)(2,1)S(1)}, bf16[64,1024]{1,0:T(8,128)(2,1)S(1)}, u32[]{:S(2)}, u32[]{:S(2)}) collective-permute-start(bf16[64,1024]{1,0:T(8,128)(2,1)S(1)} %collective-permute-done.4), channel_id=1, source_target_pairs={{0,8},{8,16},{16,24},{24,32},{32,40},{40,48},{48,56},{56,64},{64,7... | collective-permute-start | bytes 393224 | tf_op jit(solution)/shard_map/ppermute | solution.py:16
  26.1 10.0 %collective-permute-start.1 = (bf16[64,1024]{1,0:T(8,128)(2,1)S(1)}, bf16[64,1024]{1,0:T(8,128)(2,1)S(1)}, u32[]{:S(2)}, u32[]{:S(2)}) collective-permute-start(bf16[64,1024]{1,0:T(8,128)(2,1)S(1)} %collective-permute-done), channel_id=1, source_target_pairs={{0,8},{8,16},{16,24},{24,32},{32,40},{40,48},{48,56},{56,64},{64,7... | collective-permute-start | bytes 393224 | tf_op jit(solution)/shard_map/ppermute | solution.py:16
  34.0 10.0 %collective-permute-start.6 = (bf16[64,1024]{1,0:T(8,128)(2,1)S(1)}, bf16[64,1024]{1,0:T(8,128)(2,1)S(1)}, u32[]{:S(2)}, u32[]{:S(2)}) collective-permute-start(bf16[64,1024]{1,0:T(8,128)(2,1)S(1)} %collective-permute-done.5), channel_id=1, source_target_pairs={{0,8},{8,16},{16,24},{24,32},{32,40},{40,48},{48,56},{56,64},{64,7... | collective-permute-start | bytes 393224 | tf_op jit(solution)/shard_map/ppermute | solution.py:16
  36.1 10.0 %collective-permute-start.2 = (bf16[64,1024]{1,0:T(8,128)(2,1)S(1)}, bf16[64,1024]{1,0:T(8,128)(2,1)S(1)}, u32[]{:S(2)}, u32[]{:S(2)}) collective-permute-start(bf16[64,1024]{1,0:T(8,128)(2,1)S(1)} %collective-permute-done.1), channel_id=1, source_target_pairs={{0,8},{8,16},{16,24},{24,32},{32,40},{40,48},{48,56},{56,64},{64,7... | collective-permute-start | bytes 393224 | tf_op jit(solution)/shard_map/ppermute | solution.py:16
  44.0 10.0 %collective-permute-start.7 = (bf16[64,1024]{1,0:T(8,128)(2,1)S(1)}, bf16[64,1024]{1,0:T(8,128)(2,1)S(1)}, u32[]{:S(2)}, u32[]{:S(2)}) collective-permute-start(bf16[64,1024]{1,0:T(8,128)(2,1)S(1)} %collective-permute-done.6), channel_id=1, source_target_pairs={{0,8},{8,16},{16,24},{24,32},{32,40},{40,48},{48,56},{56,64},{64,7... | collective-permute-start | bytes 393224 | tf_op jit(solution)/shard_map/ppermute | solution.py:16
  46.0 10.0 %collective-permute-start.3 = (bf16[64,1024]{1,0:T(8,128)(2,1)S(1)}, bf16[64,1024]{1,0:T(8,128)(2,1)S(1)}, u32[]{:S(2)}, u32[]{:S(2)}) collective-permute-start(bf16[64,1024]{1,0:T(8,128)(2,1)S(1)} %collective-permute-done.2), channel_id=1, source_target_pairs={{0,8},{8,16},{16,24},{24,32},{32,40},{40,48},{48,56},{56,64},{64,7... | collective-permute-start | bytes 393224 | tf_op jit(solution)/shard_map/ppermute | solution.py:16
  54.2 41.9 %copy-start.7 = (bf16[320,256]{0,1:T(8,128)(2,1)}, bf16[320,256]{0,1:T(8,128)(2,1)S(1)}, u32[]{:S(2)}) copy-start(bf16[320,256]{0,1:T(8,128)(2,1)S(1)} %copy.73) | copy-start | bytes 491524
  54.4 37.9 %copy-start.9 = (bf16[320,256]{0,1:T(8,128)(2,1)}, bf16[320,256]{0,1:T(8,128)(2,1)S(1)}, u32[]{:S(2)}) copy-start(bf16[320,256]{0,1:T(8,128)(2,1)S(1)} %copy.82) | copy-start | bytes 491524
  54.6 33.4 %copy-start.10 = (bf16[320,256]{0,1:T(8,128)(2,1)}, bf16[320,256]{0,1:T(8,128)(2,1)S(1)}, u32[]{:S(2)}) copy-start(bf16[320,256]{0,1:T(8,128)(2,1)S(1)} %copy.79) | copy-start | bytes 491524
  54.8 29.5 %copy-start.12 = (bf16[320,256]{0,1:T(8,128)(2,1)}, bf16[320,256]{0,1:T(8,128)(2,1)S(1)}, u32[]{:S(2)}) copy-start(bf16[320,256]{0,1:T(8,128)(2,1)S(1)} %copy.76) | copy-start | bytes 491524
  56.3 6.4 %copy-start.29 = (bf16[320,256]{0,1:T(8,128)(2,1)}, bf16[320,256]{0,1:T(8,128)(2,1)S(1)}, u32[]{:S(2)}) copy-start(bf16[320,256]{0,1:T(8,128)(2,1)S(1)} %copy.72) | copy-start | bytes 491524
  57.9 27.2 %copy-start.15 = (f32[4,128,320]{1,2,0:T(8,128)}, f32[4,128,320]{1,2,0:T(8,128)S(1)}, u32[]{:S(2)}) copy-start(f32[4,128,320]{1,2,0:T(8,128)S(1)} %get-tuple-element.41) | copy-start | bytes 1966084
  65.3 121.2 %reduce-scatter.15.cloned.1.call-start = ((), (), s32[]{:S(2)}) async-start(), calls=%async_computation.7 | async-start | bytes 294912
  97.9 8.3 %collective-permute-start.12 = (bf16[64,1024]{1,0:T(8,128)(2,1)}, bf16[64,1024]{1,0:T(8,128)(2,1)}, u32[]{:S(2)}, u32[]{:S(2)}) collective-permute-start(bf16[64,1024]{1,0:T(8,128)(2,1)} %slice.154), channel_id=1, source_target_pairs={{0,504},{8,0},{16,8},{24,16},{32,24},{40,32},{48,40},{56,48},{64,5... | collective-permute-start | bytes 393224 | tf_op jit(solution)/shard_map/ppermute | solution.py:16
  104.3 6.8 %collective-permute-start.8 = (bf16[64,1024]{1,0:T(8,128)(2,1)S(1)}, bf16[64,1024]{1,0:T(8,128)(2,1)S(1)}, u32[]{:S(2)}, u32[]{:S(2)}) collective-permute-start(bf16[64,1024]{1,0:T(8,128)(2,1)S(1)} %slice.155), channel_id=1, source_target_pairs={{0,504},{8,0},{16,8},{24,16},{32,24},{40,32},{48,40},{56,48},{64,5... | collective-permute-start | bytes 393224 | tf_op jit(solution)/shard_map/ppermute | solution.py:16
  107.2 9.1 %collective-permute-start.13 = (bf16[64,1024]{1,0:T(8,128)(2,1)S(1)}, bf16[64,1024]{1,0:T(8,128)(2,1)S(1)}, u32[]{:S(2)}, u32[]{:S(2)}) collective-permute-start(bf16[64,1024]{1,0:T(8,128)(2,1)S(1)} %fusion.19), channel_id=1, source_target_pairs={{0,504},{8,0},{16,8},{24,16},{32,24},{40,32},{48,40},{56,48},{64,5... | collective-permute-start | bytes 393224 | tf_op jit(solution)/shard_map/ppermute | solution.py:16
  111.2 10.0 %collective-permute-start.9 = (bf16[64,1024]{1,0:T(8,128)(2,1)S(1)}, bf16[64,1024]{1,0:T(8,128)(2,1)S(1)}, u32[]{:S(2)}, u32[]{:S(2)}) collective-permute-start(bf16[64,1024]{1,0:T(8,128)(2,1)S(1)} %fusion.23), channel_id=1, source_target_pairs={{0,504},{8,0},{16,8},{24,16},{32,24},{40,32},{48,40},{56,48},{64,5... | collective-permute-start | bytes 393224 | tf_op jit(solution)/shard_map/ppermute | solution.py:16
  116.3 10.0 %collective-permute-start.14 = (bf16[64,1024]{1,0:T(8,128)(2,1)S(1)}, bf16[64,1024]{1,0:T(8,128)(2,1)S(1)}, u32[]{:S(2)}, u32[]{:S(2)}) collective-permute-start(bf16[64,1024]{1,0:T(8,128)(2,1)S(1)} %fusion.18), channel_id=1, source_target_pairs={{0,504},{8,0},{16,8},{24,16},{32,24},{40,32},{48,40},{56,48},{64,5... | collective-permute-start | bytes 393224 | tf_op jit(solution)/shard_map/ppermute | solution.py:16
  121.2 10.0 %collective-permute-start.10 = (bf16[64,1024]{1,0:T(8,128)(2,1)S(1)}, bf16[64,1024]{1,0:T(8,128)(2,1)S(1)}, u32[]{:S(2)}, u32[]{:S(2)}) collective-permute-start(bf16[64,1024]{1,0:T(8,128)(2,1)S(1)} %fusion.22), channel_id=1, source_target_pairs={{0,504},{8,0},{16,8},{24,16},{32,24},{40,32},{48,40},{56,48},{64,5... | collective-permute-start | bytes 393224 | tf_op jit(solution)/shard_map/ppermute | solution.py:16
  126.3 10.6 %collective-permute-start.15 = (bf16[64,1024]{1,0:T(8,128)(2,1)S(1)}, bf16[64,1024]{1,0:T(8,128)(2,1)S(1)}, u32[]{:S(2)}, u32[]{:S(2)}) collective-permute-start(bf16[64,1024]{1,0:T(8,128)(2,1)S(1)} %fusion.17), channel_id=1, source_target_pairs={{0,504},{8,0},{16,8},{24,16},{32,24},{40,32},{48,40},{56,48},{64,5... | collective-permute-start | bytes 393224 | tf_op jit(solution)/shard_map/ppermute | solution.py:16
  131.9 7.9 %collective-permute-start.11 = (bf16[64,1024]{1,0:T(8,128)(2,1)}, bf16[64,1024]{1,0:T(8,128)(2,1)}, u32[]{:S(2)}, u32[]{:S(2)}) collective-permute-start(bf16[64,1024]{1,0:T(8,128)(2,1)} %fusion.21), channel_id=1, source_target_pairs={{0,504},{8,0},{16,8},{24,16},{32,24},{40,32},{48,40},{56,48},{64,5... | collective-permute-start | bytes 393224 | tf_op jit(solution)/shard_map/ppermute | solution.py:16
  137.7 5.9 %copy-start.11 = (bf16[320,256]{0,1:T(8,128)(2,1)S(1)}, bf16[320,256]{0,1:T(8,128)(2,1)}, u32[]{:S(2)}) copy-start(bf16[320,256]{0,1:T(8,128)(2,1)} %copy-done.10) | copy-start | bytes 491524
  139.5 93.8 %reduce-scatter.13.cloned.1.call-start = ((), (), s32[]{:S(2)}) async-start(), calls=%async_computation.6 | async-start | bytes 294912
  141.6 4.9 %copy-start.3 = (bf16[4,128,320]{1,2,0:T(8,128)(2,1)S(1)}, bf16[4,128,320]{1,2,0:T(8,128)(2,1)}, u32[]{:S(2)}) copy-start(bf16[4,128,320]{1,2,0:T(8,128)(2,1)} %copy-done.2) | copy-start | bytes 983044
  141.6 308.0 %reduce-scatter.17.cloned.1.call-start = ((), (), s32[]{:S(2)}) async-start(), calls=%async_computation.8 | async-start | bytes 532480
  (30 other events, 68.4 us)
Sparse Core Ops, SparseCore 0:
  10.1 69.3 all-gather.1
  82.3 52.4 reduce-scatter.10
  139.7 46.8 reduce-scatter.14
  189.2 44.0 reduce-scatter.12
  237.7 211.8 reduce-scatter.16
where the time goes:
time: 459 us; the launch traced here: 458 us
  waiting for transfers between devices  337 us (73%)
  starting transfers between devices  50.4 us (11%)
  local copies, waits for them, and re-layouts  27.3 us (6%)
  matrix products  19.8 us (4%)
  between operations  14.7 us (3%)
  other arithmetic  8.21 us (2%)
    unnamed x8, waiting for transfers between devices  296 us
    ppermute x16, starting transfers between devices, shifted(): return lax.ppermute(value, axis, pairs)  50.2 us
    ppermute x16, waiting for transfers between devices, shifted(): return lax.ppermute(value, axis, pairs)  26.7 us
    unnamed x97, local copies, waits for them, and re-layouts  14.1 us
    all_gather x1, waiting for transfers between devices, local(): full_weight = lax.all_gather(out_weight, 'tgt', axis=0, tiled=True)  14.1 us
  transfers between devices with their start and end apart: 21, of which 12 were waited for; matrix products, arithmetic and copies ran while one was open for 11% of the time, Pallas kernels for 0%

commit v1 on v0

--- a/solution.py
+++ b/solution.py
@@ -64,7 +64,10 @@
 
 
 def local(queries, keys, values, out_weight, out_grad):
-    full_weight = lax.all_gather(out_weight, "tgt", axis=0, tiled=True)
+    size = lax.axis_size("tgt")
+    blocks = jnp.stack([out_weight for _ in range(size)])
+    blocks = lax.all_to_all(blocks, "tgt", split_axis=0, concat_axis=0)
+    full_weight = jnp.concatenate(blocks, axis=0)
     current = (keys, values)
     key_list = [keys]
     value_list = [values]

time: 459 us -> 478 us (1.041)
  waiting for transfers between devices: 337 us -> 294 us
  local copies, waits for them, and re-layouts: 27.3 us -> 59.2 us
  matrix products: 19.8 us -> 38.6 us
  starting transfers between devices: 50.4 us -> 59.3 us
    unnamed x8 -> x7, waiting for transfers between devices: 296 us -> 276 us
    all_gather x1 -> x0, waiting for transfers between devices: 14.1 us -> none  [local(): full_weight = lax.all_gather(out_weight, 'tgt', axis=0, tiled=True)]
    all_to_all x0 -> x1, starting transfers between devices: none -> 9.44 us  [local(): blocks = lax.all_to_all(blocks, 'tgt', split_axis=0, concat_axis=0)]
    ppermute x16, waiting for transfers between devices: 26.7 us -> 18.4 us  [shifted(): return lax.ppermute(value, axis, pairs)]
    dot_general x4, matrix products: 2.3 us -> 9.12 us  [head_block(): jnp.einsum('hrj,rhd->jhd', probs_low, grad_heads, preferred_element_type=...]
    reshape x4, local copies, waits for them, and re-layouts: 1.34 us -> 7.54 us  [head_block(): value_part.reshape(width, group_heads * HD)]
    unnamed x97 -> x95, local copies, waits for them, and re-layouts: 14.1 us -> 18.8 us
  transfers between devices with their start and end apart: 21 -> 21, of which waited for: 12 -> 10; matrix products, arithmetic and copies ran while one was open for 11% -> 21% of each run, Pallas kernels for 0% -> 0%
where the time goes in v1:
time: 478 us; the launch traced here: 476 us
  waiting for transfers between devices  294 us (62%)
  starting transfers between devices  59.3 us (12%)
  local copies, waits for them, and re-layouts  59.2 us (12%)
  matrix products  38.6 us (8%)
  between operations  14.5 us (3%)
  other arithmetic  10.4 us (2%)
    unnamed x7, waiting for transfers between devices  276 us
    ppermute x16, starting transfers between devices, shifted(): return lax.ppermute(value, axis, pairs)  49.8 us
    unnamed x95, local copies, waits for them, and re-layouts  18.8 us
    ppermute x16, waiting for transfers between devices, shifted(): return lax.ppermute(value, axis, pairs)  18.4 us
  transfers between devices with their start and end apart: 21, of which 10 were waited for; matrix products, arithmetic and copies ran while one was open for 21% of the time, Pallas kernels for 0%

profile of v1, /device:TPU:8, one launch (start us, length us, event | category | flops | bytes accessed | tf_op | source)
XLA Modules:
  0.0 476.3 jit_solution(2669578371132946056)
XLA Ops:
  7.2 2.6 stack.2
  9.8 9.4 %all-to-all-start = ((bf16[8,128,1024]{2,1,0:T(8,128)(2,1)}), bf16[8,128,1024]{2,1,0:T(8,128)(2,1)S(1)}, u32[]{:S(2)}, u32[]{:S(2)}) async-start(bf16[8,128,1024]{2,1,0:T(8,128)(2,1)} %stack.2), calls=%async_computation | async-start | bytes 4194304 | tf_op jit(solution)/shard_map/all_to_all | solution.py:69
  19.2 1.9 collective-permute-start
  21.2 1.9 collective-permute-start.4
  26.8 4.3 collective-permute-done
  31.1 1.9 collective-permute-start.1
  34.6 1.9 collective-permute-start.5
  37.4 3.9 collective-permute-done.1
  41.3 1.9 collective-permute-start.2
  44.8 1.9 collective-permute-start.6
  46.7 4.4 collective-permute-done.2
  51.2 1.9 collective-permute-start.3
  54.8 1.9 collective-permute-start.7
  57.6 3.4 collective-permute-done.3
  68.2 2.2 fusion.50
  75.8 2.2 fusion.51
  84.3 2.0 convolution_convert_fusion
  114.9 4.0 collective-permute-start.8
  118.9 2.3 fusion.24
  123.1 2.3 fusion.27
  127.3 2.2 fusion.30
  131.4 2.3 fusion.33
  137.1 1.9 collective-permute-start.12
  140.0 1.9 collective-permute-start.9
  142.0 7.0 %collective-permute-start.13 = (bf16[64,1024]{1,0:T(8,128)(2,1)S(1)}, bf16[64,1024]{1,0:T(8,128)(2,1)S(1)}, u32[]{:S(2)}, u32[]{:S(2)}) collective-permute-start(bf16[64,1024]{1,0:T(8,128)(2,1)S(1)} %fusion.19), channel_id=1, source_target_pairs={{0,504},{8,0},{16,8},{24,16},{32,24},{40,32},{48,40},{56,48},{64,5... | collective-permute-start | bytes 393224 | tf_op jit(solution)/shard_map/ppermute | solution.py:16
  149.1 2.8 collective-permute-start.10
  151.9 7.0 %collective-permute-start.14 = (bf16[64,1024]{1,0:T(8,128)(2,1)S(1)}, bf16[64,1024]{1,0:T(8,128)(2,1)S(1)}, u32[]{:S(2)}, u32[]{:S(2)}) collective-permute-start(bf16[64,1024]{1,0:T(8,128)(2,1)S(1)} %fusion.18), channel_id=1, source_target_pairs={{0,504},{8,0},{16,8},{24,16},{32,24},{40,32},{48,40},{56,48},{64,5... | collective-permute-start | bytes 393224 | tf_op jit(solution)/shard_map/ppermute | solution.py:16
  159.0 2.8 collective-permute-start.11
  162.5 7.0 %collective-permute-start.15 = (bf16[64,1024]{1,0:T(8,128)(2,1)}, bf16[64,1024]{1,0:T(8,128)(2,1)}, u32[]{:S(2)}, u32[]{:S(2)}) collective-permute-start(bf16[64,1024]{1,0:T(8,128)(2,1)} %fusion.17), channel_id=1, source_target_pairs={{0,504},{8,0},{16,8},{24,16},{32,24},{40,32},{48,40},{56,48},{64,5... | collective-permute-start | bytes 393224 | tf_op jit(solution)/shard_map/ppermute | solution.py:16
  189.5 15.4 %reduce-scatter.13.cloned.1.call-done = bf16[128,64]{1,0:T(8,128)(2,1)} async-done(((bf16[1024,64]{1,0:T(8,128)(2,1)}), bf16[128,64]{1,0:T(8,128)(2,1)}) %reduce-scatter.13.cloned.1.call-update) | async-done | bytes 16400
  206.3 45.5 %reduce-scatter.15.cloned.1.call-done = bf16[128,64]{1,0:T(8,128)(2,1)} async-done(((bf16[1024,64]{1,0:T(8,128)(2,1)}), bf16[128,64]{1,0:T(8,128)(2,1)}) %reduce-scatter.15.cloned.1.call-update) | async-done | bytes 16400
  253.3 214.9 %reduce-scatter.17.cloned.1.call-done = f32[16,128]{1,0:T(8,128)} async-done(((f32[1024,128]{1,0:T(8,128)}), f32[16,128]{1,0:T(8,128)}) %reduce-scatter.17.cloned.1.call-update) | async-done | bytes 8208
  (188 shorter events, 92.5 us)
Async XLA Ops:
  7.2 77.1 %copy-start = (bf16[128,1024]{1,0:T(8,128)(2,1)S(1)}, bf16[128,1024]{1,0:T(8,128)(2,1)}, u32[]{:S(2)}) copy-start(bf16[128,1024]{1,0:T(8,128)(2,1)} %param.9) | copy-start | bytes 786436
  9.8 9.4 %copy-start.35 = (bf16[64,1024]{1,0:T(8,128)(2,1)S(1)}, bf16[64,1024]{1,0:T(8,128)(2,1)}, u32[]{:S(2)}) copy-start(bf16[64,1024]{1,0:T(8,128)(2,1)} %param.7) | copy-start | bytes 393220
  9.8 11.4 %copy-start.36 = (bf16[64,1024]{1,0:T(8,128)(2,1)S(1)}, bf16[64,1024]{1,0:T(8,128)(2,1)}, u32[]{:S(2)}) copy-start(bf16[64,1024]{1,0:T(8,128)(2,1)} %param.6) | copy-start | bytes 393220
  9.8 13.3 %copy-start.29 = (bf16[128,1024]{1,0:T(8,128)(2,1)S(1)}, bf16[128,1024]{1,0:T(8,128)(2,1)}, u32[]{:S(2)}) copy-start(bf16[128,1024]{1,0:T(8,128)(2,1)} %param.5) | copy-start | bytes 786436
  9.8 76.6 %all-to-all-start = ((bf16[8,128,1024]{2,1,0:T(8,128)(2,1)}), bf16[8,128,1024]{2,1,0:T(8,128)(2,1)S(1)}, u32[]{:S(2)}, u32[]{:S(2)}) async-start(bf16[8,128,1024]{2,1,0:T(8,128)(2,1)} %stack.2), calls=%async_computation | async-start | bytes 4194304 | tf_op jit(solution)/shard_map/all_to_all | solution.py:69
  19.2 163.3 %reduce-scatter.11.cloned.1.call-start = ((), (), s32[]{:S(2)}) async-start(), calls=%async_computation.5 | async-start | bytes 2359296 | tf_op jit(solution)/shard_map/reduce_scatter | solution.py:120
  19.2 11.8 %collective-permute-start = (bf16[64,1024]{1,0:T(8,128)(2,1)S(1)}, bf16[64,1024]{1,0:T(8,128)(2,1)}, u32[]{:S(2)}, u32[]{:S(2)}) collective-permute-start(bf16[64,1024]{1,0:T(8,128)(2,1)S(1)} %copy-done.35), channel_id=1, source_target_pairs={{0,8},{8,16},{16,24},{24,32},{32,40},{40,48},{48,56},{56,64},{64,7... | collective-permute-start | bytes 393224 | tf_op jit(solution)/shard_map/ppermute | solution.py:16
  21.2 13.4 %collective-permute-start.4 = (bf16[64,1024]{1,0:T(8,128)(2,1)S(1)}, bf16[64,1024]{1,0:T(8,128)(2,1)}, u32[]{:S(2)}, u32[]{:S(2)}) collective-permute-start(bf16[64,1024]{1,0:T(8,128)(2,1)S(1)} %copy-done.36), channel_id=1, source_target_pairs={{0,8},{8,16},{16,24},{24,32},{32,40},{40,48},{48,56},{56,64},{64,7... | collective-permute-start | bytes 393224 | tf_op jit(solution)/shard_map/ppermute | solution.py:16
  31.1 10.2 %collective-permute-start.1 = (bf16[64,1024]{1,0:T(8,128)(2,1)}, bf16[64,1024]{1,0:T(8,128)(2,1)S(1)}, u32[]{:S(2)}, u32[]{:S(2)}) collective-permute-start(bf16[64,1024]{1,0:T(8,128)(2,1)} %collective-permute-done), channel_id=1, source_target_pairs={{0,8},{8,16},{16,24},{24,32},{32,40},{40,48},{48,56},{56,64},{64,7... | collective-permute-start | bytes 393224 | tf_op jit(solution)/shard_map/ppermute | solution.py:16
  34.6 10.2 %collective-permute-start.5 = (bf16[64,1024]{1,0:T(8,128)(2,1)}, bf16[64,1024]{1,0:T(8,128)(2,1)S(1)}, u32[]{:S(2)}, u32[]{:S(2)}) collective-permute-start(bf16[64,1024]{1,0:T(8,128)(2,1)} %collective-permute-done.4), channel_id=1, source_target_pairs={{0,8},{8,16},{16,24},{24,32},{32,40},{40,48},{48,56},{56,64},{64,7... | collective-permute-start | bytes 393224 | tf_op jit(solution)/shard_map/ppermute | solution.py:16
  41.3 9.9 %collective-permute-start.2 = (bf16[64,1024]{1,0:T(8,128)(2,1)S(1)}, bf16[64,1024]{1,0:T(8,128)(2,1)S(1)}, u32[]{:S(2)}, u32[]{:S(2)}) collective-permute-start(bf16[64,1024]{1,0:T(8,128)(2,1)S(1)} %collective-permute-done.1), channel_id=1, source_target_pairs={{0,8},{8,16},{16,24},{24,32},{32,40},{40,48},{48,56},{56,64},{64,7... | collective-permute-start | bytes 393224 | tf_op jit(solution)/shard_map/ppermute | solution.py:16
  44.8 10.0 %collective-permute-start.6 = (bf16[64,1024]{1,0:T(8,128)(2,1)S(1)}, bf16[64,1024]{1,0:T(8,128)(2,1)}, u32[]{:S(2)}, u32[]{:S(2)}) collective-permute-start(bf16[64,1024]{1,0:T(8,128)(2,1)S(1)} %collective-permute-done.5), channel_id=1, source_target_pairs={{0,8},{8,16},{16,24},{24,32},{32,40},{40,48},{48,56},{56,64},{64,7... | collective-permute-start | bytes 393224 | tf_op jit(solution)/shard_map/ppermute | solution.py:16
  51.2 9.9 %collective-permute-start.3 = (bf16[64,1024]{1,0:T(8,128)(2,1)S(1)}, bf16[64,1024]{1,0:T(8,128)(2,1)S(1)}, u32[]{:S(2)}, u32[]{:S(2)}) collective-permute-start(bf16[64,1024]{1,0:T(8,128)(2,1)S(1)} %collective-permute-done.2), channel_id=1, source_target_pairs={{0,8},{8,16},{16,24},{24,32},{32,40},{40,48},{48,56},{56,64},{64,7... | collective-permute-start | bytes 393224 | tf_op jit(solution)/shard_map/ppermute | solution.py:16
  54.8 10.5 %collective-permute-start.7 = (bf16[64,1024]{1,0:T(8,128)(2,1)}, bf16[64,1024]{1,0:T(8,128)(2,1)}, u32[]{:S(2)}, u32[]{:S(2)}) collective-permute-start(bf16[64,1024]{1,0:T(8,128)(2,1)} %collective-permute-done.6), channel_id=1, source_target_pairs={{0,8},{8,16},{16,24},{24,32},{32,40},{40,48},{48,56},{56,64},{64,7... | collective-permute-start | bytes 393224 | tf_op jit(solution)/shard_map/ppermute | solution.py:16
  71.0 13.3 %copy-start.15 = (bf16[4,64,128]{2,1,0:T(8,128)(2,1)}, bf16[4,64,128]{2,1,0:T(8,128)(2,1)S(1)}, u32[]{:S(2)}) copy-start(bf16[4,64,128]{2,1,0:T(8,128)(2,1)S(1)} %convolution_convert_fusion.7) | copy-start | bytes 196612
  72.9 6.7 %copy-start.9 = (bf16[320,256]{0,1:T(8,128)(2,1)}, bf16[320,256]{0,1:T(8,128)(2,1)S(1)}, u32[]{:S(2)}) copy-start(bf16[320,256]{0,1:T(8,128)(2,1)S(1)} %copy.79) | copy-start | bytes 491524
  75.8 7.9 %copy-start.6 = (bf16[320,256]{0,1:T(8,128)(2,1)}, bf16[320,256]{0,1:T(8,128)(2,1)S(1)}, u32[]{:S(2)}) copy-start(bf16[320,256]{0,1:T(8,128)(2,1)S(1)} %copy.73) | copy-start | bytes 491524
  79.6 4.7 copy-start.17
  86.3 118.6 %reduce-scatter.13.cloned.1.call-start = ((), (), s32[]{:S(2)}) async-start(), calls=%async_computation.6 | async-start | bytes 294912
  114.9 24.1 %collective-permute-start.8 = (bf16[64,1024]{1,0:T(8,128)(2,1)}, bf16[64,1024]{1,0:T(8,128)(2,1)}, u32[]{:S(2)}, u32[]{:S(2)}) collective-permute-start(bf16[64,1024]{1,0:T(8,128)(2,1)} %slice.155), channel_id=1, source_target_pairs={{0,504},{8,0},{16,8},{24,16},{32,24},{40,32},{48,40},{56,48},{64,5... | collective-permute-start | bytes 393224 | tf_op jit(solution)/shard_map/ppermute | solution.py:16
  137.1 24.7 %copy-start.3 = (f32[320,1024]{1,0:T(8,128)}, f32[320,1024]{1,0:T(8,128)S(1)}, u32[]{:S(2)}) copy-start(f32[320,1024]{1,0:T(8,128)S(1)} %pad_maximum_fusion.1) | copy-start | bytes 3932164
  137.1 4.8 %collective-permute-start.12 = (bf16[64,1024]{1,0:T(8,128)(2,1)S(1)}, bf16[64,1024]{1,0:T(8,128)(2,1)S(1)}, u32[]{:S(2)}, u32[]{:S(2)}) collective-permute-start(bf16[64,1024]{1,0:T(8,128)(2,1)S(1)} %slice.154), channel_id=1, source_target_pairs={{0,504},{8,0},{16,8},{24,16},{32,24},{40,32},{48,40},{56,48},{64,5... | collective-permute-start | bytes 393224 | tf_op jit(solution)/shard_map/ppermute | solution.py:16
  140.0 9.0 %collective-permute-start.9 = (bf16[64,1024]{1,0:T(8,128)(2,1)S(1)}, bf16[64,1024]{1,0:T(8,128)(2,1)S(1)}, u32[]{:S(2)}, u32[]{:S(2)}) collective-permute-start(bf16[64,1024]{1,0:T(8,128)(2,1)S(1)} %fusion.23), channel_id=1, source_target_pairs={{0,504},{8,0},{16,8},{24,16},{32,24},{40,32},{48,40},{56,48},{64,5... | collective-permute-start | bytes 393224 | tf_op jit(solution)/shard_map/ppermute | solution.py:16
  142.0 9.9 %collective-permute-start.13 = (bf16[64,1024]{1,0:T(8,128)(2,1)S(1)}, bf16[64,1024]{1,0:T(8,128)(2,1)S(1)}, u32[]{:S(2)}, u32[]{:S(2)}) collective-permute-start(bf16[64,1024]{1,0:T(8,128)(2,1)S(1)} %fusion.19), channel_id=1, source_target_pairs={{0,504},{8,0},{16,8},{24,16},{32,24},{40,32},{48,40},{56,48},{64,5... | collective-permute-start | bytes 393224 | tf_op jit(solution)/shard_map/ppermute | solution.py:16
  149.1 9.9 %collective-permute-start.10 = (bf16[64,1024]{1,0:T(8,128)(2,1)S(1)}, bf16[64,1024]{1,0:T(8,128)(2,1)S(1)}, u32[]{:S(2)}, u32[]{:S(2)}) collective-permute-start(bf16[64,1024]{1,0:T(8,128)(2,1)S(1)} %fusion.22), channel_id=1, source_target_pairs={{0,504},{8,0},{16,8},{24,16},{32,24},{40,32},{48,40},{56,48},{64,5... | collective-permute-start | bytes 393224 | tf_op jit(solution)/shard_map/ppermute | solution.py:16
  151.9 9.9 %collective-permute-start.14 = (bf16[64,1024]{1,0:T(8,128)(2,1)S(1)}, bf16[64,1024]{1,0:T(8,128)(2,1)S(1)}, u32[]{:S(2)}, u32[]{:S(2)}) collective-permute-start(bf16[64,1024]{1,0:T(8,128)(2,1)S(1)} %fusion.18), channel_id=1, source_target_pairs={{0,504},{8,0},{16,8},{24,16},{32,24},{40,32},{48,40},{56,48},{64,5... | collective-permute-start | bytes 393224 | tf_op jit(solution)/shard_map/ppermute | solution.py:16
  159.0 10.5 %collective-permute-start.11 = (bf16[64,1024]{1,0:T(8,128)(2,1)S(1)}, bf16[64,1024]{1,0:T(8,128)(2,1)S(1)}, u32[]{:S(2)}, u32[]{:S(2)}) collective-permute-start(bf16[64,1024]{1,0:T(8,128)(2,1)S(1)} %fusion.21), channel_id=1, source_target_pairs={{0,504},{8,0},{16,8},{24,16},{32,24},{40,32},{48,40},{56,48},{64,5... | collective-permute-start | bytes 393224 | tf_op jit(solution)/shard_map/ppermute | solution.py:16
  162.5 9.8 %collective-permute-start.15 = (bf16[64,1024]{1,0:T(8,128)(2,1)}, bf16[64,1024]{1,0:T(8,128)(2,1)}, u32[]{:S(2)}, u32[]{:S(2)}) collective-permute-start(bf16[64,1024]{1,0:T(8,128)(2,1)} %fusion.17), channel_id=1, source_target_pairs={{0,504},{8,0},{16,8},{24,16},{32,24},{40,32},{48,40},{56,48},{64,5... | collective-permute-start | bytes 393224 | tf_op jit(solution)/shard_map/ppermute | solution.py:16
  172.0 79.9 %reduce-scatter.15.cloned.1.call-start = ((), (), s32[]{:S(2)}) async-start(), calls=%async_computation.7 | async-start | bytes 294912
  175.8 292.5 %reduce-scatter.17.cloned.1.call-start = ((), (), s32[]{:S(2)}) async-start(), calls=%async_computation.8 | async-start | bytes 532480
  179.1 7.2 %copy-start.5 = (bf16[4,128,320]{1,2,0:T(8,128)(2,1)S(1)}, bf16[4,128,320]{1,2,0:T(8,128)(2,1)}, u32[]{:S(2)}) copy-start(bf16[4,128,320]{1,2,0:T(8,128)(2,1)} %copy-done.4) | copy-start | bytes 983044
  181.0 5.4 %copy-start.7 = (bf16[320,256]{0,1:T(8,128)(2,1)S(1)}, bf16[320,256]{0,1:T(8,128)(2,1)}, u32[]{:S(2)}) copy-start(bf16[320,256]{0,1:T(8,128)(2,1)} %copy-done.6) | copy-start | bytes 491524
  (29 other events, 65.2 us)
Sparse Core Ops, SparseCore 0:
  86.4 48.4 reduce-scatter.10
  172.1 32.7 reduce-scatter.12
  207.7 44.1 reduce-scatter.14
  256.3 211.8 reduce-scatter.16
